TPU v7x, 32 devices: a whole 2x2x4 slice. The times are simulated.
32 devices in a mesh: seq: 16 (over z, y, x), grp: 2 (over core).
Axes of the slice: x: 2, y: 2, z: 4, core: 2. Of those that a mesh axis runs over, the one named last changes fastest.
Arguments:
- key_rows: bfloat16 [32768, 4096], P('seq', 'grp')
- probe_ints: int32 [4096, 512], P('grp'), may hold values from -2 to 2
- rank_keep: int32 [1], replicated, may hold values from 128 to 511
Outputs:
- latents: float32 [32768, 512], P('seq', 'grp')
- latent_basis: float32 [512, 4096], P('seq', 'grp')
All inputs are finite; a program needn't handle non-finite values.
Results may differ from a plain program's by a relative error of at most 0.00098.
Values may be sent and summed in bfloat16 or wider, within the bound.
A program may use at most 128 MiB of HBM per device.

v0:
```python
import math
import jax
import jax.numpy as jnp
from jax import lax
from jax.sharding import PartitionSpec as P


def on_device(key_rows, probe_ints, rank_keep):
    seq_count = lax.axis_size("seq")
    tokens = key_rows.shape[0] * seq_count
    root_tokens = math.sqrt(tokens)
    probes = (probe_ints.astype(jnp.float32) * 0.015625).astype(jnp.bfloat16)
    whole_keys = lax.all_gather(key_rows, "grp", axis=1, tiled=True)
    whole_probes = lax.all_gather(probes, "grp", axis=0, tiled=True)
    sketch = jnp.dot(whole_keys, whole_probes, preferred_element_type=jnp.float32)
    contract = (((0,), (0,)), ((), ()))
    local_gram = lax.dot_general(sketch, sketch, contract, precision=lax.Precision.HIGHEST)
    gram_matrix = lax.psum(local_gram, "seq")
    lower_factor = jnp.linalg.cholesky(gram_matrix)
    identity = jnp.eye(gram_matrix.shape[0], dtype=jnp.float32)
    inverse = lax.linalg.triangular_solve(lower_factor, identity, left_side=True, lower=True)
    orthonormal = jnp.dot(sketch, inverse.T, precision=lax.Precision.HIGHEST) * root_tokens
    probe_count = orthonormal.shape[1]
    part_width = probe_count // lax.axis_size("grp")
    first_column = lax.axis_index("grp") * part_width
    columns = first_column + jnp.arange(part_width)
    own_columns = lax.dynamic_slice_in_dim(orthonormal, first_column, part_width, 1)
    latents = jnp.where(columns[None, :] < rank_keep[0], own_columns, jnp.float32(0.0))
    rounded = orthonormal.astype(jnp.bfloat16)
    rows_out = probe_count // seq_count
    summed = lax.psum_scatter(
        lax.dot_general(rounded, key_rows, contract, preferred_element_type=jnp.float32),
        "seq",
        scatter_dimension=0,
        tiled=True,
    )
    row_index = lax.axis_index("seq") * rows_out + jnp.arange(rows_out)
    latent_basis = jnp.where(
        row_index[:, None] < rank_keep[0], summed / root_tokens, jnp.float32(0.0)
    )
    return (latents, latent_basis)


def solution(mesh):
    in_specs = (P("seq", "grp"), P("grp", None), P())
    out_specs = (P("seq", "grp"), P("seq", "grp"))
    return jax.shard_map(
        on_device, mesh=mesh, in_specs=in_specs, out_specs=out_specs, check_vma=False
    )
```

profile of v0, /device:TPU:0, one launch (start us, length us, event | category | flops | bytes accessed | tf_op | source)
XLA Modules:
  0.0 463.2 jit_solution(5321967595677841850)
XLA Ops:
  7.2 4.1 multiply_convert_fusion
  12.1 15.7 %all-gather.3.cloned.1.call-done = bf16[4096,512]{1,0:T(8,128)(2,1)} async-done(((bf16[2048,512]{1,0:T(8,128)(2,1)}), bf16[4096,512]{1,0:T(8,128)(2,1)}) %all-gather.3.cloned.1.call-update) | async-done | bytes 4194320 | tf_op jit(solution)/shard_map/all_gather | solution.py:14
  27.8 32.8 %all-gather.5.cloned.1.call-done = bf16[2048,4096]{1,0:T(8,128)(2,1)} async-done(((bf16[2048,2048]{1,0:T(8,128)(2,1)}), bf16[2048,4096]{1,0:T(8,128)(2,1)}) %all-gather.5.cloned.1.call-update) | async-done | bytes 16777232 | tf_op jit(solution)/shard_map/all_gather | solution.py:13
  60.7 13.0 %fusion.42 = f32[512,2048]{1,0:T(8,128)S(1)} fusion(bf16[4096,512]{1,0:T(8,128)(2,1)} %all-gather.3.cloned.1.call-done, bf16[2048,4096]{1,0:T(8,128)(2,1)} %all-gather.5.cloned.1.call-done), kind=kOutput, calls=%fused_computation.84 | convolution fusion | flops 8589934592 | bytes 25165824 | tf_op jit(solution)/shard_map/dot_general | solution.py:15
  73.7 1.9 copy-done
  75.7 7.7 %fusion.43 = f32[512,512]{0,1:T(8,128)} fusion(f32[512,2048]{1,0:T(8,128)S(1)} %fusion.42), kind=kOutput, calls=%fused_computation.85 | convolution fusion | flops 6442450944 | bytes 5242880 | tf_op jit(solution)/shard_map/dot_general | solution.py:17
  84.5 111.9 %all-reduce.3.cloned.1.call-done = f32[512,512]{0,1:T(8,128)} async-done(((f32[512,512]{0,1:T(8,128)}), f32[512,512]{0,1:T(8,128)}) %all-reduce.3.cloned.1.call-update) | async-done | bytes 1048592 | tf_op jit(solution)/shard_map/psum | solution.py:18
  199.5 11.7 %cholesky.104 = f32[128,128]{1,0:T(8,128)S(1)} custom-call(f32[128,128]{1,0:T(8,128)S(1)} %cholesky.266), custom_call_target="Cholesky" | custom-call | tf_op jit(solution)/shard_map/jit(cholesky)/cholesky | solution.py:19
  211.2 9.8 %custom-call.30 = f32[1,128,128]{1,2,0:T(8,128)S(1)} custom-call(f32[1,128,128]{2,1,0:T(8,128)S(1)} %get-tuple-element.29), custom_call_target="InvertDiagBlocksLowerTriangular" | custom-call | tf_op jit(solution)/shard_map/jit(cholesky)/cholesky | solution.py:19
  221.8 11.7 %cholesky.217 = f32[128,128]{1,0:T(8,128)S(1)} custom-call(f32[128,128]{1,0:T(8,128)S(1)} %cholesky.270), custom_call_target="Cholesky" | custom-call | tf_op jit(solution)/shard_map/jit(cholesky)/cholesky | solution.py:19
  233.6 10.2 %custom-call.31 = f32[1,128,128]{1,2,0:T(8,128)S(1)} custom-call(f32[1,128,128]{2,1,0:T(8,128)S(1)} %get-tuple-element.26), custom_call_target="InvertDiagBlocksLowerTriangular" | custom-call | tf_op jit(solution)/shard_map/jit(cholesky)/cholesky | solution.py:19
  244.4 11.7 %cholesky.238 = f32[128,128]{1,0:T(8,128)S(1)} custom-call(f32[128,128]{1,0:T(8,128)S(1)} %cholesky.275), custom_call_target="Cholesky" | custom-call | tf_op jit(solution)/shard_map/jit(cholesky)/cholesky | solution.py:19
  256.8 9.8 %custom-call.32 = f32[1,128,128]{1,2,0:T(8,128)S(1)} custom-call(f32[1,128,128]{2,1,0:T(8,128)S(1)} %get-tuple-element.23), custom_call_target="InvertDiagBlocksLowerTriangular" | custom-call | tf_op jit(solution)/shard_map/jit(cholesky)/cholesky | solution.py:19
  267.3 11.7 %cholesky.255 = f32[128,128]{1,0:T(8,128)S(1)} custom-call(f32[128,128]{1,0:T(8,128)S(1)} %convolution_subtract_fusion.5), custom_call_target="Cholesky" | custom-call | tf_op jit(solution)/shard_map/jit(cholesky)/cholesky | solution.py:19
  283.3 10.3 %while.1 = (s32[]{:T(128)}, f32[512,512]{1,0:T(8,128)S(1)}, s32[4,2]{0,1:T(2,128)S(1)}, f32[4,128,128]{2,1,0:T(8,128)}, s32[]{:T(128)}) while((s32[]{:T(128)}, f32[512,512]{1,0:T(8,128)S(1)}, s32[4,2]{0,1:T(2,128)S(1)}, f32[4,128,128]{2,1,0:T(8,128)}, s32[]{:T(128)}) %tuple.31), condition=%wide.while_cond, body=%wide.while_body.sunk | while | flops 2 | bytes 132705 | solution.py:21
  283.9 2.0 bitcast_dynamic-update-slice_fusion.2
  286.4 2.0 bitcast_dynamic-update-slice_fusion.2
  289.0 2.0 bitcast_dynamic-update-slice_fusion.2
  291.6 2.0 bitcast_dynamic-update-slice_fusion.2
  293.6 40.1 %custom-call.33 = f32[4,128,128]{1,2,0:T(8,128)S(1)} custom-call(f32[4,128,128]{2,1,0:T(8,128)} %get-tuple-element.9), custom_call_target="InvertDiagBlocksLowerTriangular" | custom-call | tf_op jit(solution)/shard_map/triangular_solve | solution.py:21
  337.7 14.6 %convolution_multiply_fusion = f32[2048,512]{1,0:T(8,128)S(1)} fusion(f32[512,2048]{1,0:T(8,128)S(1)} %copy-done.1, f32[128,512]{1,0:T(8,128)S(1)} %fusion.29, f32[128,512]{1,0:T(8,128)S(1)} %fusion.30, f32[128,512]{1,0:T(8,128)S(1)} %fusion.32, f32[128,512]{1,0:T(8,128)S(1)} %fusion.20), kind=kOutput, calls=%fused_computation.3 | convolution fusion | flops 6444285952 | bytes 9437184 | tf_op jit(solution)/shard_map/dot_general | solution.py:22
  354.2 6.1 %fusion = f32[512,2048]{1,0:T(8,128)} fusion(bf16[2048,2048]{1,0:T(8,128)(2,1)S(1)} %bitcast.58, f32[2048,512]{1,0:T(8,128)S(1)} %convolution_multiply_fusion), kind=kOutput, calls=%fused_computation.4 | convolution fusion | flops 4296015872 | bytes 16777216 | tf_op jit(solution)/shard_map/dot_general | solution.py:32
  361.0 3.1 dynamic-slice_select_fusion
  364.1 90.6 %reduce-scatter.2.cloned.1.call-done = f32[32,2048]{1,0:T(8,128)} async-done(((f32[512,2048]{1,0:T(8,128)}), f32[32,2048]{1,0:T(8,128)}) %reduce-scatter.2.cloned.1.call-update) | async-done | bytes 262160 | tf_op jit(solution)/shard_map/reduce_scatter | solution.py:31
  (61 shorter events, 19.5 us)
Async XLA Ops:
  7.2 20.7 %all-gather.3.cloned.1.call-start = ((), (), s32[]{:S(2)}) async-start(), calls=%async_computation.1 | async-start | bytes 6291456 | tf_op jit(solution)/shard_map/all_gather | solution.py:14
  11.3 49.4 %all-gather.5.cloned.1.call-start = ((), (), s32[]{:S(2)}) async-start(), calls=%async_computation.2 | async-start | bytes 25165824 | tf_op jit(solution)/shard_map/all_gather | solution.py:13
  12.1 184.4 %all-reduce.3.cloned.1.call-start = ((), (), s32[]{:S(2)}) async-start(), calls=%async_computation.3 | async-start | bytes 2097152 | tf_op jit(solution)/shard_map/psum | solution.py:18
  73.7 1.9 copy-start
  83.4 371.3 %reduce-scatter.2.cloned.1.call-start = ((), (), s32[]{:S(2)}) async-start(), calls=%async_computation.4 | async-start | bytes 4456448 | tf_op jit(solution)/shard_map/reduce_scatter | solution.py:31
  333.7 4.0 copy-start.1
  336.6 17.6 %slice-start = ((s8[8388608]{0:T(1024)(128)(4,1)}), s8[4194304]{0:T(1024)(128)(4,1)S(1)}, s32[]{:S(2)}) async-start(s8[8388608]{0:T(1024)(128)(4,1)} %bitcast.57), calls=%async_computation.5 | async-start | bytes 8388608
  337.7 16.5 %slice-start.1 = ((s8[8388608]{0:T(1024)(128)(4,1)}), s8[4194304]{0:T(1024)(128)(4,1)S(1)}, s32[]{:S(2)}) async-start(s8[8388608]{0:T(1024)(128)(4,1)} %bitcast.57), calls=%async_computation.6 | async-start | bytes 8388608
  352.3 1.9 copy-start.2
Sparse Core Ops, SparseCore 0:
  11.4 16.3 all-gather.2
  29.4 31.2 all-gather.4
  83.5 112.8 all-reduce.2
  360.4 94.2 reduce-scatter.1
where the time goes:
time: 471 us; the launch traced here: 463 us
  waiting for transfers between devices  252 us (54%)
  other arithmetic  130 us (28%)
  matrix products  47.2 us (10%)
  between operations  17.5 us (4%)
  local copies, waits for them, and re-layouts  15.8 us (3%)
    psum x1, waiting for transfers between devices, on_device(): gram_matrix = lax.psum(local_gram, 'seq')  112 us
    reduce_scatter x1, waiting for transfers between devices, on_device(): lax.psum_scatter(lax.dot_general(rounded, key_rows, contract, preferred_e...  90.6 us
    another operation x14, other arithmetic, on_device(): lower_factor = jnp.linalg.cholesky(gram_matrix)  79 us
    another operation x3, other arithmetic, on_device(): lax.linalg.triangular_solve(lower_factor, identity, left_side=True, lower...  40.3 us
    all_gather x1, waiting for transfers between devices, on_device(): whole_keys = lax.all_gather(key_rows, 'grp', axis=1, tiled=True)  32.8 us
    all_gather x1, waiting for transfers between devices, on_device(): whole_probes = lax.all_gather(probes, 'grp', axis=0, tiled=True)  15.7 us
    dot_general x1, matrix products, on_device(): jnp.dot(sketch, inverse.T, precision=lax.Precision.HIGHEST) * root_tokens  14.6 us
    dot_general x1, matrix products, on_device(): jnp.dot(whole_keys, whole_probes, preferred_element_type=jnp.float32)  13 us
  transfers between devices with their start and end apart: 4, of which 4 were waited for; matrix products, arithmetic and copies ran while one was open for 1% of the time, Pallas kernels for 0%

commit v1 on v0

--- a/solution.py
+++ b/solution.py
@@ -15,7 +15,8 @@
     sketch = jnp.dot(whole_keys, whole_probes, preferred_element_type=jnp.float32)
     contract = (((0,), (0,)), ((), ()))
     local_gram = lax.dot_general(sketch, sketch, contract, precision=lax.Precision.HIGHEST)
-    gram_matrix = lax.psum(local_gram, "seq")
+    block_last = lax.all_gather(local_gram, axis_name="seq")
+    gram_matrix = jnp.sum(block_last, 0)
     lower_factor = jnp.linalg.cholesky(gram_matrix)
     identity = jnp.eye(gram_matrix.shape[0], dtype=jnp.float32)
     inverse = lax.linalg.triangular_solve(lower_factor, identity, left_side=True, lower=True)

time: 471 us -> 562 us (1.19)
  waiting for transfers between devices: 252 us -> 332 us
  other arithmetic: 130 us -> 136 us
    all_gather x0 -> x1, waiting for transfers between devices: none -> 192 us  [on_device(): block_last = lax.all_gather(local_gram, axis_name='seq')]
    psum x1 -> x0, waiting for transfers between devices: 112 us -> none  [on_device(): gram_matrix = lax.psum(local_gram, 'seq')]
    reduce_sum x0 -> x1, other arithmetic: none -> 7.91 us  [on_device(): gram_matrix = jnp.sum(block_last, 0)]
where the time goes in v1:
time: 562 us; the launch traced here: 554 us
  waiting for transfers between devices  332 us (59%)
  other arithmetic  136 us (24%)
  matrix products  52 us (9%)
  between operations  17.5 us (3%)
  local copies, waits for them, and re-layouts  16.2 us (3%)
    all_gather x1, waiting for transfers between devices, on_device(): block_last = lax.all_gather(local_gram, axis_name='seq')  192 us
    reduce_scatter x1, waiting for transfers between devices, on_device(): lax.psum_scatter(lax.dot_general(rounded, key_rows, contract, preferred_e...  89.7 us
    another operation x14, other arithmetic, on_device(): lower_factor = jnp.linalg.cholesky(gram_matrix)  79 us
    another operation x3, other arithmetic, on_device(): lax.linalg.triangular_solve(lower_factor, identity, left_side=True, lower...  40.3 us
    all_gather x1, waiting for transfers between devices, on_device(): whole_keys = lax.all_gather(key_rows, 'grp', axis=1, tiled=True)  32.8 us
    all_gather x1, waiting for transfers between devices, on_device(): whole_probes = lax.all_gather(probes, 'grp', axis=0, tiled=True)  15.7 us
    dot_general x1, matrix products, on_device(): jnp.dot(sketch, inverse.T, precision=lax.Precision.HIGHEST) * root_tokens  14.6 us
    dot_general x1, matrix products, on_device(): jnp.dot(whole_keys, whole_probes, preferred_element_type=jnp.float32)  13 us
  transfers between devices with their start and end apart: 4, of which 4 were waited for; matrix products, arithmetic and copies ran while one was open for 1% of the time, Pallas kernels for 0%

profile of v1, /device:TPU:0, one launch (start us, length us, event | category | flops | bytes accessed | tf_op | source)
XLA Modules:
  0.0 554.1 jit_solution(5761405247406659829)
XLA Ops:
  7.2 4.1 multiply_convert_fusion
  12.1 15.7 %all-gather.5.cloned.1.call-done = bf16[4096,512]{1,0:T(8,128)(2,1)} async-done(((bf16[2048,512]{1,0:T(8,128)(2,1)}), bf16[4096,512]{1,0:T(8,128)(2,1)}) %all-gather.5.cloned.1.call-update) | async-done | bytes 4194320 | tf_op jit(solution)/shard_map/all_gather | solution.py:14
  27.8 32.8 %all-gather.7.cloned.1.call-done = bf16[2048,4096]{1,0:T(8,128)(2,1)} async-done(((bf16[2048,2048]{1,0:T(8,128)(2,1)}), bf16[2048,4096]{1,0:T(8,128)(2,1)}) %all-gather.7.cloned.1.call-update) | async-done | bytes 16777232 | tf_op jit(solution)/shard_map/all_gather | solution.py:13
  60.7 13.0 %fusion.42 = f32[512,2048]{1,0:T(8,128)S(1)} fusion(bf16[4096,512]{1,0:T(8,128)(2,1)} %all-gather.5.cloned.1.call-done, bf16[2048,4096]{1,0:T(8,128)(2,1)} %all-gather.7.cloned.1.call-done), kind=kOutput, calls=%fused_computation.84 | convolution fusion | flops 8589934592 | bytes 25165824 | tf_op jit(solution)/shard_map/dot_general | solution.py:15
  75.7 7.9 %fusion.43 = f32[512,512]{1,0:T(8,128)} fusion(f32[512,2048]{1,0:T(8,128)S(1)} %fusion.42), kind=kOutput, calls=%fused_computation.85 | convolution fusion | flops 6442450944 | bytes 5242880 | tf_op jit(solution)/shard_map/dot_general | solution.py:17
  84.0 192.5 %all-gather.9.cloned.1.call-done = f32[8192,512]{1,0:T(8,128)} async-done(((f32[512,512]{1,0:T(8,128)}), f32[8192,512]{1,0:T(8,128)}) %all-gather.9.cloned.1.call-update) | async-done | bytes 16777232 | tf_op jit(solution)/shard_map/all_gather | solution.py:18
  276.5 7.9 %reduce_sum.9 = f32[512,512]{1,0:T(8,128)S(1)} reduce(f32[16,512,512]{2,1,0:T(8,128)} %bitcast.58, f32[]{:T(128)} %constant.153.clone.1), dimensions={0}, to_apply=%region_0.0 | reduce | flops 3932160 | bytes 17825796 | tf_op jit(solution)/shard_map/reduce_sum | solution.py:19
  285.9 11.7 %cholesky.104 = f32[128,128]{1,0:T(8,128)S(1)} custom-call(f32[128,128]{1,0:T(8,128)S(1)} %cholesky.266), custom_call_target="Cholesky" | custom-call | tf_op jit(solution)/shard_map/jit(cholesky)/cholesky | solution.py:20
  297.8 9.8 %custom-call.30 = f32[1,128,128]{1,2,0:T(8,128)S(1)} custom-call(f32[1,128,128]{2,1,0:T(8,128)S(1)} %get-tuple-element.29), custom_call_target="InvertDiagBlocksLowerTriangular" | custom-call | tf_op jit(solution)/shard_map/jit(cholesky)/cholesky | solution.py:20
  310.2 12.1 %cholesky.217 = f32[128,128]{1,0:T(8,128)S(1)} custom-call(f32[128,128]{1,0:T(8,128)S(1)} %cholesky.270), custom_call_target="Cholesky" | custom-call | tf_op jit(solution)/shard_map/jit(cholesky)/cholesky | solution.py:20
  322.3 9.8 %custom-call.31 = f32[1,128,128]{1,2,0:T(8,128)S(1)} custom-call(f32[1,128,128]{2,1,0:T(8,128)S(1)} %get-tuple-element.26), custom_call_target="InvertDiagBlocksLowerTriangular" | custom-call | tf_op jit(solution)/shard_map/jit(cholesky)/cholesky | solution.py:20
  333.7 11.7 %cholesky.238 = f32[128,128]{1,0:T(8,128)S(1)} custom-call(f32[128,128]{1,0:T(8,128)S(1)} %cholesky.275), custom_call_target="Cholesky" | custom-call | tf_op jit(solution)/shard_map/jit(cholesky)/cholesky | solution.py:20
  346.2 9.8 %custom-call.32 = f32[1,128,128]{1,2,0:T(8,128)S(1)} custom-call(f32[1,128,128]{2,1,0:T(8,128)S(1)} %get-tuple-element.23), custom_call_target="InvertDiagBlocksLowerTriangular" | custom-call | tf_op jit(solution)/shard_map/jit(cholesky)/cholesky | solution.py:20
  357.4 11.9 %cholesky.255 = f32[128,128]{1,0:T(8,128)S(1)} custom-call(f32[128,128]{1,0:T(8,128)S(1)} %convolution_subtract_fusion.5), custom_call_target="Cholesky" | custom-call | tf_op jit(solution)/shard_map/jit(cholesky)/cholesky | solution.py:20
  373.3 10.9 %while.1 = (s32[]{:T(128)}, f32[512,512]{1,0:T(8,128)S(1)}, s32[4,2]{0,1:T(2,128)S(1)}, f32[4,128,128]{2,1,0:T(8,128)}, s32[]{:T(128)}) while((s32[]{:T(128)}, f32[512,512]{1,0:T(8,128)S(1)}, s32[4,2]{0,1:T(2,128)S(1)}, f32[4,128,128]{2,1,0:T(8,128)}, s32[]{:T(128)}) %tuple.31), condition=%wide.while_cond, body=%wide.while_body.sunk | while | flops 2 | bytes 132705 | solution.py:22
  374.0 2.1 bitcast_dynamic-update-slice_fusion.2
  376.7 2.1 bitcast_dynamic-update-slice_fusion.2
  379.5 2.1 bitcast_dynamic-update-slice_fusion.2
  382.2 2.1 bitcast_dynamic-update-slice_fusion.2
  384.2 40.1 %custom-call.33 = f32[4,128,128]{1,2,0:T(8,128)S(1)} custom-call(f32[4,128,128]{2,1,0:T(8,128)} %get-tuple-element.9), custom_call_target="InvertDiagBlocksLowerTriangular" | custom-call | tf_op jit(solution)/shard_map/triangular_solve | solution.py:22
  429.5 14.6 %convolution_multiply_fusion = f32[2048,512]{1,0:T(8,128)S(1)} fusion(f32[512,2048]{1,0:T(8,128)S(1)} %copy-done.1, f32[128,512]{1,0:T(8,128)S(1)} %fusion.29, f32[128,512]{1,0:T(8,128)S(1)} %fusion.30, f32[128,512]{1,0:T(8,128)S(1)} %fusion.32, f32[128,512]{1,0:T(8,128)S(1)} %fusion.20), kind=kOutput, calls=%fused_computation.3 | convolution fusion | flops 6444285952 | bytes 9437184 | tf_op jit(solution)/shard_map/dot_general | solution.py:23
  446.0 6.1 %fusion = f32[512,2048]{1,0:T(8,128)} fusion(bf16[2048,2048]{1,0:T(8,128)(2,1)S(1)} %bitcast.60, f32[2048,512]{1,0:T(8,128)S(1)} %convolution_multiply_fusion), kind=kOutput, calls=%fused_computation.4 | convolution fusion | flops 4296015872 | bytes 16777216 | tf_op jit(solution)/shard_map/dot_general | solution.py:33
  452.8 3.1 dynamic-slice_select_fusion
  455.8 89.7 %reduce-scatter.2.cloned.1.call-done = f32[32,2048]{1,0:T(8,128)} async-done(((f32[512,2048]{1,0:T(8,128)}), f32[32,2048]{1,0:T(8,128)}) %reduce-scatter.2.cloned.1.call-update) | async-done | bytes 262160 | tf_op jit(solution)/shard_map/reduce_scatter | solution.py:32
  (66 shorter events, 24.0 us)
Async XLA Ops:
  7.2 20.7 %all-gather.5.cloned.1.call-start = ((), (), s32[]{:S(2)}) async-start(), calls=%async_computation.1 | async-start | bytes 6291456 | tf_op jit(solution)/shard_map/all_gather | solution.py:14
  11.3 49.4 %all-gather.7.cloned.1.call-start = ((), (), s32[]{:S(2)}) async-start(), calls=%async_computation.2 | async-start | bytes 25165824 | tf_op jit(solution)/shard_map/all_gather | solution.py:13
  12.1 264.4 %all-gather.9.cloned.1.call-start = ((), (), s32[]{:S(2)}) async-start(), calls=%async_computation.4 | async-start | bytes 17825792 | tf_op jit(solution)/shard_map/all_gather | solution.py:18
  73.7 1.9 copy-start
  83.5 462.0 %reduce-scatter.2.cloned.1.call-start = ((), (), s32[]{:S(2)}) async-start(), calls=%async_computation.3 | async-start | bytes 4456448 | tf_op jit(solution)/shard_map/reduce_scatter | solution.py:32
  285.0 1.0 copy-start.3
  424.4 0.7 copy-start.4
  424.4 5.1 copy-start.1
  427.2 18.8 %slice-start = ((s8[8388608]{0:T(1024)(128)(4,1)}), s8[4194304]{0:T(1024)(128)(4,1)S(1)}, s32[]{:S(2)}) async-start(s8[8388608]{0:T(1024)(128)(4,1)} %bitcast.59), calls=%async_computation.5 | async-start | bytes 8388608
  429.5 16.5 %slice-start.1 = ((s8[8388608]{0:T(1024)(128)(4,1)}), s8[4194304]{0:T(1024)(128)(4,1)S(1)}, s32[]{:S(2)}) async-start(s8[8388608]{0:T(1024)(128)(4,1)} %bitcast.59), calls=%async_computation.6 | async-start | bytes 8388608
  444.1 1.9 copy-start.2
Sparse Core Ops, SparseCore 0:
  11.4 16.3 all-gather.4
  29.4 31.2 all-gather.6
  83.7 192.7 all-gather.8
  452.2 93.3 reduce-scatter.1
